TPU v7x, 512 devices: a whole 4x8x8 slice. The times are simulated.
512 devices in a mesh: gx: 32 (over x_hi, y, core), gy: 16 (over x_lo, z).
Axes of the slice: x: 4 (x_hi: 2, x_lo: 2; x = x_hi * 2 + x_lo), y: 8, z: 8, core: 2. Of those that a mesh axis runs over, the one named last changes fastest.
Arguments:
- rhs: float32 [32, 125, 2048], P('gx', None, 'gy'), may hold values from -6 to 6
- inverse: bfloat16 [32, 125, 125, 2048], P('gx', None, None, 'gy')
- weights: float32 [32, 4, 2048], P('gx', None, 'gy'), may hold values from 0.12 to 0.3
- neighbours: int32 [32, 4, 2048], P('gx', None, 'gy'), may hold values from 0 to 383, as said below
- send_lists: int32 [32, 4, 1024], P('gx', None, 'gy'), may hold values from 0 to 127
- coloring: int32 [32, 16], P('gx', 'gy'), may hold values from 0 to 3, as said below
Outputs:
- solution: float32 [32, 125, 2048], P('gx', None, 'gy')
- norms: float32 [2], replicated
Inputs may be any that keep to these rules, and one draw needn't show every extreme that they name: `coloring`: the color of subdomain (i, j) depends only on i mod 2 and j mod 2, and the four parity classes have four different colors; which class has which color varies. `neighbours`: slots below 128 are the subdomain's own faces, the rest the received intersection faces in the order of the steps; every received slot is used by some face.
All inputs are finite; a program needn't handle non-finite values.
Results may differ from a plain program's by a relative error of at most 0.0055.
Values sent between devices are 32-bit elements; how exact they have to be, the bound alone decides.
A program may use at most 64 MiB of HBM per device.

v0:
```python
import jax
import jax.numpy as jnp
from jax import lax
from jax.sharding import Mesh
from jax.sharding import PartitionSpec as P

SWEEPS = 2
GX = ("gx_0", "gx_1", "gx_2")
GY = ("gy_0", "gy_1")
GX_GY = ("gx_0", "gx_1", "gx_2", "gy_0", "gy_1")


def extended_2(cells, sides, width):
    for axis, dim in sides:
        count = lax.axis_size(axis)
        ends = count - 1
        head = lax.slice_in_dim(cells, 0, width, axis=dim)
        tail = lax.slice_in_dim(cells, cells.shape[dim] - width, cells.shape[dim], axis=dim)
        cells = jnp.concatenate(
            [
                lax.ppermute(tail, axis, [(i, (i + 1) % count) for i in range(ends)]),
                cells,
                lax.ppermute(head, axis, [((i + 1) % count, i) for i in range(ends)]),
            ],
            axis=dim,
        )
    return cells


def by_axis(array, axes):
    for axis in axes:
        array = lax.psum(array, axis)
    return array


def gather_margin(solution, sending):
    packs = [jnp.take(solution, sending[side], axis=1) for side in range(4)]
    rows_pair = jnp.stack([packs[1], packs[0]])
    rows_full = extended_2(rows_pair, ((GX, 0),), 1)
    cols_pair = jnp.stack([packs[3], packs[2]])
    cols_full = extended_2(cols_pair, ((GY, 0),), 1)
    below, above = (rows_full[0], rows_full[3])
    left, right_side = (cols_full[0], cols_full[3])
    return jnp.concatenate([solution, below, above, left, right_side], axis=1)


def body(rhs, inverse, weights, neighbours, send_lists, coloring):
    right = rhs[0]
    blocks = inverse[0]
    coupling = weights[0]
    slots = neighbours[0]
    sending = send_lists[0]
    own_color = coloring[0, 0]
    solution = jnp.zeros(right.shape, jnp.float32)
    locals_list = []

    def update(operands):
        extended, current = operands
        couple = jnp.zeros_like(current)
        for k in range(coupling.shape[0]):
            couple = couple + coupling[k][None, :] * jnp.take(extended, slots[k], axis=1)
        source = (right + couple).astype(jnp.bfloat16)
        candidate = jnp.einsum("ijf,jf->if", blocks, source, preferred_element_type=jnp.float32)
        delta = candidate - current
        return (candidate, jnp.sum(delta * delta))

    def unchanged(operands):
        return (operands[1], jnp.zeros((), jnp.float32))

    for sweep in range(SWEEPS):
        squares = jnp.zeros((), jnp.float32)
        for color in range(4):
            extended = gather_margin(solution, sending)
            solution, increment = lax.cond(
                own_color == color, update, unchanged, (extended, solution)
            )
            squares = squares + increment
        locals_list.append(squares)
    totals = by_axis(jnp.stack(locals_list), GX_GY)
    norms = jnp.sqrt(totals)
    return (solution[None], norms)


def solution(mesh):
    split = Mesh(mesh.devices.reshape(2, 8, 2, 2, 8), ("gx_0", "gx_1", "gx_2", "gy_0", "gy_1"))
    in_specs = (
        P(GX, None, GY),
        P(GX, None, None, GY),
        P(GX, None, GY),
        P(GX, None, GY),
        P(GX, None, GY),
        P(GX, GY),
    )
    out_specs = (P(GX, None, GY), P())
    return jax.shard_map(body, mesh=split, in_specs=in_specs, out_specs=out_specs, check_vma=False)
```

profile of v0, /device:TPU:6, one launch (start us, length us, event | category | flops | bytes accessed | tf_op | source)
XLA Modules:
  0.0 306.6 jit_solution(6864680266955408566)
XLA Ops:
  4.8 7.2 %collective-permute-start.1 = (f32[1,125,64]{1,2,0:T(8,128)S(1)}, f32[1,125,64]{1,2,0:T(8,128)S(1)}, u32[]{:S(2)}, u32[]{:S(2)}) collective-permute-start(f32[1,125,64]{1,2,0:T(8,128)S(1)} %select_bitcast_fusion.30), channel_id=1, source_target_pairs={{16,0},{32,16},{48,32},{64,48},{80,64},{96,80},{112,96},{128,112},... | collective-permute-start | bytes 96008 | tf_op jit(solution)/shard_map/ppermute | solution.py:23
  17.7 8.8 %collective-permute-start.3 = (f32[1,125,64]{1,2,0:T(8,128)S(1)}, f32[1,125,64]{1,2,0:T(8,128)S(1)}, u32[]{:S(2)}, u32[]{:S(2)}) collective-permute-start(f32[1,125,64]{1,2,0:T(8,128)S(1)} %select_bitcast_fusion.28), channel_id=1, source_target_pairs={{1,0},{2,1},{3,2},{4,3},{5,4},{6,5},{7,6},{8,7},{9,8},{10,9},{11,1... | collective-permute-start | bytes 96008 | tf_op jit(solution)/shard_map/ppermute | solution.py:23
  36.2 16.2 %collective-permute-start.4 = (f32[1,125,64]{1,2,0:T(8,128)S(1)}, f32[1,125,64]{1,2,0:T(8,128)S(1)}, u32[]{:S(2)}, u32[]{:S(2)}) collective-permute-start(f32[1,125,64]{1,2,0:T(8,128)S(1)} %select_bitcast_fusion.27), channel_id=1, source_target_pairs={{0,16},{16,32},{32,48},{48,64},{64,80},{80,96},{96,112},{112,128},... | collective-permute-start | bytes 96008 | tf_op jit(solution)/shard_map/ppermute | solution.py:21
  52.5 6.2 %collective-permute-start.5 = (f32[1,125,64]{1,2,0:T(8,128)S(1)}, f32[1,125,64]{1,2,0:T(8,128)S(1)}, u32[]{:S(2)}, u32[]{:S(2)}) collective-permute-start(f32[1,125,64]{1,2,0:T(8,128)S(1)} %select_bitcast_fusion.26), channel_id=1, source_target_pairs={{16,0},{32,16},{48,32},{64,48},{80,64},{96,80},{112,96},{128,112},... | collective-permute-start | bytes 96008 | tf_op jit(solution)/shard_map/ppermute | solution.py:23
  60.7 6.0 %collective-permute-start.7 = (f32[1,125,64]{1,2,0:T(8,128)S(1)}, f32[1,125,64]{1,2,0:T(8,128)S(1)}, u32[]{:S(2)}, u32[]{:S(2)}) collective-permute-start(f32[1,125,64]{1,2,0:T(8,128)S(1)} %select_bitcast_fusion.24), channel_id=1, source_target_pairs={{1,0},{2,1},{3,2},{4,3},{5,4},{6,5},{7,6},{8,7},{9,8},{10,9},{11,1... | collective-permute-start | bytes 96008 | tf_op jit(solution)/shard_map/ppermute | solution.py:23
  68.3 11.6 %conditional.9 = (f32[125,128]{1,0:T(8,128)}, f32[]{:T(128)}) conditional(s32[]{:T(128)} %bitcast.107, f32[125,128]{1,0:T(8,128)} %get-tuple-element.202, (f32[4,128]{1,0:T(4,128)}, s32[4,128]{1,0:T(4,128)}, f32[125,384]{0,1:T(8,128)S(1)}, f32[125,128]{0,1:T(8,128)S(1)}, bf16[125,125,128]{2,1,0:T(8,128)(2,1)}, /*index=5*/f32[125,128]{0,1:T(8,128)}) %tuple.266), branch_computations={%region_3.0_spmd, %region_4.0_spmd} | conditional | flops 6263167 | bytes 5439764 | solution.py:74
  85.4 7.2 %collective-permute-start.9 = (f32[1,125,64]{1,2,0:T(8,128)S(1)}, f32[1,125,64]{1,2,0:T(8,128)S(1)}, u32[]{:S(2)}, u32[]{:S(2)}) collective-permute-start(f32[1,125,64]{1,2,0:T(8,128)S(1)} %select_bitcast_fusion.22), channel_id=1, source_target_pairs={{16,0},{32,16},{48,32},{64,48},{80,64},{96,80},{112,96},{128,112},... | collective-permute-start | bytes 96008 | tf_op jit(solution)/shard_map/ppermute | solution.py:23
  94.7 6.0 %collective-permute-start.11 = (f32[1,125,64]{1,2,0:T(8,128)S(1)}, f32[1,125,64]{1,2,0:T(8,128)S(1)}, u32[]{:S(2)}, u32[]{:S(2)}) collective-permute-start(f32[1,125,64]{1,2,0:T(8,128)S(1)} %select_bitcast_fusion.20), channel_id=1, source_target_pairs={{1,0},{2,1},{3,2},{4,3},{5,4},{6,5},{7,6},{8,7},{9,8},{10,9},{11,1... | collective-permute-start | bytes 96008 | tf_op jit(solution)/shard_map/ppermute | solution.py:23
  109.2 7.2 %collective-permute-start.13 = (f32[1,125,64]{1,2,0:T(8,128)S(1)}, f32[1,125,64]{1,2,0:T(8,128)S(1)}, u32[]{:S(2)}, u32[]{:S(2)}) collective-permute-start(f32[1,125,64]{1,2,0:T(8,128)S(1)} %select_bitcast_fusion.18), channel_id=1, source_target_pairs={{16,0},{32,16},{48,32},{64,48},{80,64},{96,80},{112,96},{128,112},... | collective-permute-start | bytes 96008 | tf_op jit(solution)/shard_map/ppermute | solution.py:23
  116.5 9.3 %collective-permute-start.14 = (f32[1,125,64]{1,2,0:T(8,128)S(1)}, f32[1,125,64]{1,2,0:T(8,128)S(1)}, u32[]{:S(2)}, u32[]{:S(2)}) collective-permute-start(f32[1,125,64]{1,2,0:T(8,128)S(1)} %select_bitcast_fusion.17), channel_id=1, source_target_pairs={{0,1},{1,2},{2,3},{3,4},{4,5},{5,6},{6,7},{7,8},{8,9},{9,10},{10,1... | collective-permute-start | bytes 96008 | tf_op jit(solution)/shard_map/ppermute | solution.py:21
  125.9 8.3 %collective-permute-start.15 = (f32[1,125,64]{1,2,0:T(8,128)S(1)}, f32[1,125,64]{1,2,0:T(8,128)S(1)}, u32[]{:S(2)}, u32[]{:S(2)}) collective-permute-start(f32[1,125,64]{1,2,0:T(8,128)S(1)} %select_bitcast_fusion.16), channel_id=1, source_target_pairs={{1,0},{2,1},{3,2},{4,3},{5,4},{6,5},{7,6},{8,7},{9,8},{10,9},{11,1... | collective-permute-start | bytes 96008 | tf_op jit(solution)/shard_map/ppermute | solution.py:23
  142.6 7.2 %collective-permute-start.17 = (f32[1,125,64]{1,2,0:T(8,128)S(1)}, f32[1,125,64]{1,2,0:T(8,128)S(1)}, u32[]{:S(2)}, u32[]{:S(2)}) collective-permute-start(f32[1,125,64]{1,2,0:T(8,128)S(1)} %select_bitcast_fusion.14), channel_id=1, source_target_pairs={{16,0},{32,16},{48,32},{64,48},{80,64},{96,80},{112,96},{128,112},... | collective-permute-start | bytes 96008 | tf_op jit(solution)/shard_map/ppermute | solution.py:23
  152.8 8.3 %collective-permute-start.19 = (f32[1,125,64]{1,2,0:T(8,128)S(1)}, f32[1,125,64]{1,2,0:T(8,128)S(1)}, u32[]{:S(2)}, u32[]{:S(2)}) collective-permute-start(f32[1,125,64]{1,2,0:T(8,128)S(1)} %select_bitcast_fusion.12), channel_id=1, source_target_pairs={{1,0},{2,1},{3,2},{4,3},{5,4},{6,5},{7,6},{8,7},{9,8},{10,9},{11,1... | collective-permute-start | bytes 96008 | tf_op jit(solution)/shard_map/ppermute | solution.py:23
  173.7 7.4 %collective-permute-start.21 = (f32[1,125,64]{1,2,0:T(8,128)S(1)}, f32[1,125,64]{1,2,0:T(8,128)S(1)}, u32[]{:S(2)}, u32[]{:S(2)}) collective-permute-start(f32[1,125,64]{1,2,0:T(8,128)S(1)} %select_bitcast_fusion.10), channel_id=1, source_target_pairs={{16,0},{32,16},{48,32},{64,48},{80,64},{96,80},{112,96},{128,112},... | collective-permute-start | bytes 96008 | tf_op jit(solution)/shard_map/ppermute | solution.py:23
  183.1 6.0 %collective-permute-start.23 = (f32[1,125,64]{1,2,0:T(8,128)S(1)}, f32[1,125,64]{1,2,0:T(8,128)S(1)}, u32[]{:S(2)}, u32[]{:S(2)}) collective-permute-start(f32[1,125,64]{1,2,0:T(8,128)S(1)} %select_bitcast_fusion.8), channel_id=1, source_target_pairs={{1,0},{2,1},{3,2},{4,3},{5,4},{6,5},{7,6},{8,7},{9,8},{10,9},{11,1... | collective-permute-start | bytes 96008 | tf_op jit(solution)/shard_map/ppermute | solution.py:23
  190.7 10.9 %conditional.13 = (f32[125,128]{1,0:T(8,128)}, f32[]{:T(128)}) conditional(s32[]{:T(128)} %bitcast.107, f32[125,128]{1,0:T(8,128)} %get-tuple-element.175, (f32[4,128]{1,0:T(4,128)}, s32[4,128]{1,0:T(4,128)}, f32[125,384]{0,1:T(8,128)S(1)}, f32[125,128]{0,1:T(8,128)S(1)}, bf16[125,125,128]{2,1,0:T(8,128)(2,1)}, ...), branch_computations={%region_15.18_spmd, %region_16.0_spmd} | conditional | flops 6263167 | bytes 5311764 | solution.py:74
  207.0 7.2 %collective-permute-start.25 = (f32[1,125,64]{1,2,0:T(8,128)S(1)}, f32[1,125,64]{1,2,0:T(8,128)S(1)}, u32[]{:S(2)}, u32[]{:S(2)}) collective-permute-start(f32[1,125,64]{1,2,0:T(8,128)S(1)} %select_bitcast_fusion.6), channel_id=1, source_target_pairs={{16,0},{32,16},{48,32},{64,48},{80,64},{96,80},{112,96},{128,112},... | collective-permute-start | bytes 96008 | tf_op jit(solution)/shard_map/ppermute | solution.py:23
  216.4 6.0 %collective-permute-start.27 = (f32[1,125,64]{1,2,0:T(8,128)S(1)}, f32[1,125,64]{1,2,0:T(8,128)S(1)}, u32[]{:S(2)}, u32[]{:S(2)}) collective-permute-start(f32[1,125,64]{1,2,0:T(8,128)S(1)} %select_bitcast_fusion.4), channel_id=1, source_target_pairs={{1,0},{2,1},{3,2},{4,3},{5,4},{6,5},{7,6},{8,7},{9,8},{10,9},{11,1... | collective-permute-start | bytes 96008 | tf_op jit(solution)/shard_map/ppermute | solution.py:23
  230.8 7.2 %collective-permute-start.29 = (f32[1,125,64]{1,2,0:T(8,128)S(1)}, f32[1,125,64]{1,2,0:T(8,128)S(1)}, u32[]{:S(2)}, u32[]{:S(2)}) collective-permute-start(f32[1,125,64]{1,2,0:T(8,128)S(1)} %select_bitcast_fusion.2), channel_id=1, source_target_pairs={{16,0},{32,16},{48,32},{64,48},{80,64},{96,80},{112,96},{128,112},... | collective-permute-start | bytes 96008 | tf_op jit(solution)/shard_map/ppermute | solution.py:23
  238.2 9.1 %collective-permute-start.30 = (f32[1,125,64]{1,2,0:T(8,128)S(1)}, f32[1,125,64]{1,2,0:T(8,128)S(1)}, u32[]{:S(2)}, u32[]{:S(2)}) collective-permute-start(f32[1,125,64]{1,2,0:T(8,128)S(1)} %select_bitcast_fusion.1), channel_id=1, source_target_pairs={{0,1},{1,2},{2,3},{3,4},{4,5},{5,6},{6,7},{7,8},{8,9},{9,10},{10,1... | collective-permute-start | bytes 96008 | tf_op jit(solution)/shard_map/ppermute | solution.py:21
  247.4 8.4 %collective-permute-start.31 = (f32[1,125,64]{1,2,0:T(8,128)S(1)}, f32[1,125,64]{1,2,0:T(8,128)S(1)}, u32[]{:S(2)}, u32[]{:S(2)}) collective-permute-start(f32[1,125,64]{1,2,0:T(8,128)S(1)} %select_bitcast_fusion), channel_id=1, source_target_pairs={{1,0},{2,1},{3,2},{4,3},{5,4},{6,5},{7,6},{8,7},{9,8},{10,9},{11,1... | collective-permute-start | bytes 96008 | tf_op jit(solution)/shard_map/ppermute | solution.py:23
  258.9 6.4 %psum.35 = f32[2]{0:T(128)S(1)} all-reduce(f32[2]{0:T(128)S(1)} %pad_maximum_fusion), channel_id=1, replica_groups=mesh['gx_0'=2,'gx_1'=8,'gx_2'=2,'gy_0'=2,'gy_1'=8] {'gx_0'}, use_global_device_ids=true, to_apply=%region_24.27 | all-reduce | flops 2 | bytes 16 | tf_op jit(solution)/shard_map/psum | solution.py:32
  265.4 14.2 %psum.36 = f32[2]{0:T(128)S(1)} all-reduce(f32[2]{0:T(128)S(1)} %psum.35), channel_id=1, replica_groups=mesh['gx_0'=2,'gx_1'=8,'gx_2'=2,'gy_0'=2,'gy_1'=8] {'gx_1'}, use_global_device_ids=true, to_apply=%region_25.28 | all-reduce | flops 2 | bytes 16 | tf_op jit(solution)/shard_map/psum | solution.py:32
  286.9 17.7 %psum.39 = f32[2]{0:T(128)S(1)} all-reduce(f32[2]{0:T(128)S(1)} %psum.38), channel_id=1, replica_groups=mesh['gx_0'=2,'gx_1'=8,'gx_2'=2,'gy_0'=2,'gy_1'=8] {'gy_1'}, use_global_device_ids=true, to_apply=%region_28.31 | all-reduce | flops 2 | bytes 16 | tf_op jit(solution)/shard_map/psum | solution.py:32
  (205 shorter events, 123.8 us)
Async XLA Ops:
  2.2 26.0 %collective-permute-start = (f32[1,125,64]{1,2,0:T(8,128)S(1)}, f32[1,125,64]{1,2,0:T(8,128)S(1)}, u32[]{:S(2)}, u32[]{:S(2)}) collective-permute-start(f32[1,125,64]{1,2,0:T(8,128)S(1)} %select_bitcast_fusion.31), channel_id=1, source_target_pairs={{0,16},{16,32},{32,48},{48,64},{64,80},{80,96},{96,112},{112,128},... | collective-permute-start | bytes 96008 | tf_op jit(solution)/shard_map/ppermute | solution.py:21
  4.8 23.4 %collective-permute-start.1 = (f32[1,125,64]{1,2,0:T(8,128)S(1)}, f32[1,125,64]{1,2,0:T(8,128)S(1)}, u32[]{:S(2)}, u32[]{:S(2)}) collective-permute-start(f32[1,125,64]{1,2,0:T(8,128)S(1)} %select_bitcast_fusion.30), channel_id=1, source_target_pairs={{16,0},{32,16},{48,32},{64,48},{80,64},{96,80},{112,96},{128,112},... | collective-permute-start | bytes 96008 | tf_op jit(solution)/shard_map/ppermute | solution.py:23
  12.7 15.5 %collective-permute-start.2 = (f32[1,125,64]{1,2,0:T(8,128)S(1)}, f32[1,125,64]{1,2,0:T(8,128)S(1)}, u32[]{:S(2)}, u32[]{:S(2)}) collective-permute-start(f32[1,125,64]{1,2,0:T(8,128)S(1)} %select_bitcast_fusion.29), channel_id=1, source_target_pairs={{0,1},{1,2},{2,3},{3,4},{4,5},{5,6},{6,7},{7,8},{8,9},{9,10},{10,1... | collective-permute-start | bytes 96008 | tf_op jit(solution)/shard_map/ppermute | solution.py:21
  17.7 10.5 %collective-permute-start.3 = (f32[1,125,64]{1,2,0:T(8,128)S(1)}, f32[1,125,64]{1,2,0:T(8,128)S(1)}, u32[]{:S(2)}, u32[]{:S(2)}) collective-permute-start(f32[1,125,64]{1,2,0:T(8,128)S(1)} %select_bitcast_fusion.28), channel_id=1, source_target_pairs={{1,0},{2,1},{3,2},{4,3},{5,4},{6,5},{7,6},{8,7},{9,8},{10,9},{11,1... | collective-permute-start | bytes 96008 | tf_op jit(solution)/shard_map/ppermute | solution.py:23
  36.2 30.6 %collective-permute-start.4 = (f32[1,125,64]{1,2,0:T(8,128)S(1)}, f32[1,125,64]{1,2,0:T(8,128)S(1)}, u32[]{:S(2)}, u32[]{:S(2)}) collective-permute-start(f32[1,125,64]{1,2,0:T(8,128)S(1)} %select_bitcast_fusion.27), channel_id=1, source_target_pairs={{0,16},{16,32},{32,48},{48,64},{64,80},{80,96},{96,112},{112,128},... | collective-permute-start | bytes 96008 | tf_op jit(solution)/shard_map/ppermute | solution.py:21
  52.5 14.3 %collective-permute-start.5 = (f32[1,125,64]{1,2,0:T(8,128)S(1)}, f32[1,125,64]{1,2,0:T(8,128)S(1)}, u32[]{:S(2)}, u32[]{:S(2)}) collective-permute-start(f32[1,125,64]{1,2,0:T(8,128)S(1)} %select_bitcast_fusion.26), channel_id=1, source_target_pairs={{16,0},{32,16},{48,32},{64,48},{80,64},{96,80},{112,96},{128,112},... | collective-permute-start | bytes 96008 | tf_op jit(solution)/shard_map/ppermute | solution.py:23
  83.4 17.4 %collective-permute-start.8 = (f32[1,125,64]{1,2,0:T(8,128)S(1)}, f32[1,125,64]{1,2,0:T(8,128)S(1)}, u32[]{:S(2)}, u32[]{:S(2)}) collective-permute-start(f32[1,125,64]{1,2,0:T(8,128)S(1)} %select_bitcast_fusion.23), channel_id=1, source_target_pairs={{0,16},{16,32},{32,48},{48,64},{64,80},{80,96},{96,112},{112,128},... | collective-permute-start | bytes 96008 | tf_op jit(solution)/shard_map/ppermute | solution.py:21
  85.4 15.4 %collective-permute-start.9 = (f32[1,125,64]{1,2,0:T(8,128)S(1)}, f32[1,125,64]{1,2,0:T(8,128)S(1)}, u32[]{:S(2)}, u32[]{:S(2)}) collective-permute-start(f32[1,125,64]{1,2,0:T(8,128)S(1)} %select_bitcast_fusion.22), channel_id=1, source_target_pairs={{16,0},{32,16},{48,32},{64,48},{80,64},{96,80},{112,96},{128,112},... | collective-permute-start | bytes 96008 | tf_op jit(solution)/shard_map/ppermute | solution.py:23
  107.2 27.0 %collective-permute-start.12 = (f32[1,125,64]{1,2,0:T(8,128)S(1)}, f32[1,125,64]{1,2,0:T(8,128)S(1)}, u32[]{:S(2)}, u32[]{:S(2)}) collective-permute-start(f32[1,125,64]{1,2,0:T(8,128)S(1)} %select_bitcast_fusion.19), channel_id=1, source_target_pairs={{0,16},{16,32},{32,48},{48,64},{64,80},{80,96},{96,112},{112,128},... | collective-permute-start | bytes 96008 | tf_op jit(solution)/shard_map/ppermute | solution.py:21
  109.2 25.0 %collective-permute-start.13 = (f32[1,125,64]{1,2,0:T(8,128)S(1)}, f32[1,125,64]{1,2,0:T(8,128)S(1)}, u32[]{:S(2)}, u32[]{:S(2)}) collective-permute-start(f32[1,125,64]{1,2,0:T(8,128)S(1)} %select_bitcast_fusion.18), channel_id=1, source_target_pairs={{16,0},{32,16},{48,32},{64,48},{80,64},{96,80},{112,96},{128,112},... | collective-permute-start | bytes 96008 | tf_op jit(solution)/shard_map/ppermute | solution.py:23
  116.5 17.7 %collective-permute-start.14 = (f32[1,125,64]{1,2,0:T(8,128)S(1)}, f32[1,125,64]{1,2,0:T(8,128)S(1)}, u32[]{:S(2)}, u32[]{:S(2)}) collective-permute-start(f32[1,125,64]{1,2,0:T(8,128)S(1)} %select_bitcast_fusion.17), channel_id=1, source_target_pairs={{0,1},{1,2},{2,3},{3,4},{4,5},{5,6},{6,7},{7,8},{8,9},{9,10},{10,1... | collective-permute-start | bytes 96008 | tf_op jit(solution)/shard_map/ppermute | solution.py:21
  125.9 9.8 %collective-permute-start.15 = (f32[1,125,64]{1,2,0:T(8,128)S(1)}, f32[1,125,64]{1,2,0:T(8,128)S(1)}, u32[]{:S(2)}, u32[]{:S(2)}) collective-permute-start(f32[1,125,64]{1,2,0:T(8,128)S(1)} %select_bitcast_fusion.16), channel_id=1, source_target_pairs={{1,0},{2,1},{3,2},{4,3},{5,4},{6,5},{7,6},{8,7},{9,8},{10,9},{11,1... | collective-permute-start | bytes 96008 | tf_op jit(solution)/shard_map/ppermute | solution.py:23
  140.6 20.5 %collective-permute-start.16 = (f32[1,125,64]{1,2,0:T(8,128)S(1)}, f32[1,125,64]{1,2,0:T(8,128)S(1)}, u32[]{:S(2)}, u32[]{:S(2)}) collective-permute-start(f32[1,125,64]{1,2,0:T(8,128)S(1)} %select_bitcast_fusion.15), channel_id=1, source_target_pairs={{0,16},{16,32},{32,48},{48,64},{64,80},{80,96},{96,112},{112,128},... | collective-permute-start | bytes 96008 | tf_op jit(solution)/shard_map/ppermute | solution.py:21
  142.6 18.5 %collective-permute-start.17 = (f32[1,125,64]{1,2,0:T(8,128)S(1)}, f32[1,125,64]{1,2,0:T(8,128)S(1)}, u32[]{:S(2)}, u32[]{:S(2)}) collective-permute-start(f32[1,125,64]{1,2,0:T(8,128)S(1)} %select_bitcast_fusion.14), channel_id=1, source_target_pairs={{16,0},{32,16},{48,32},{64,48},{80,64},{96,80},{112,96},{128,112},... | collective-permute-start | bytes 96008 | tf_op jit(solution)/shard_map/ppermute | solution.py:23
  150.0 11.2 %collective-permute-start.18 = (f32[1,125,64]{1,2,0:T(8,128)S(1)}, f32[1,125,64]{1,2,0:T(8,128)S(1)}, u32[]{:S(2)}, u32[]{:S(2)}) collective-permute-start(f32[1,125,64]{1,2,0:T(8,128)S(1)} %select_bitcast_fusion.13), channel_id=1, source_target_pairs={{0,1},{1,2},{2,3},{3,4},{4,5},{5,6},{6,7},{7,8},{8,9},{9,10},{10,1... | collective-permute-start | bytes 96008 | tf_op jit(solution)/shard_map/ppermute | solution.py:21
  152.8 9.8 %collective-permute-start.19 = (f32[1,125,64]{1,2,0:T(8,128)S(1)}, f32[1,125,64]{1,2,0:T(8,128)S(1)}, u32[]{:S(2)}, u32[]{:S(2)}) collective-permute-start(f32[1,125,64]{1,2,0:T(8,128)S(1)} %select_bitcast_fusion.12), channel_id=1, source_target_pairs={{1,0},{2,1},{3,2},{4,3},{5,4},{6,5},{7,6},{8,7},{9,8},{10,9},{11,1... | collective-permute-start | bytes 96008 | tf_op jit(solution)/shard_map/ppermute | solution.py:23
  167.6 21.6 %collective-permute-start.20 = (f32[1,125,64]{1,2,0:T(8,128)S(1)}, f32[1,125,64]{1,2,0:T(8,128)S(1)}, u32[]{:S(2)}, u32[]{:S(2)}) collective-permute-start(f32[1,125,64]{1,2,0:T(8,128)S(1)} %select_bitcast_fusion.11), channel_id=1, source_target_pairs={{0,16},{16,32},{32,48},{48,64},{64,80},{80,96},{96,112},{112,128},... | collective-permute-start | bytes 96008 | tf_op jit(solution)/shard_map/ppermute | solution.py:21
  173.7 15.5 %collective-permute-start.21 = (f32[1,125,64]{1,2,0:T(8,128)S(1)}, f32[1,125,64]{1,2,0:T(8,128)S(1)}, u32[]{:S(2)}, u32[]{:S(2)}) collective-permute-start(f32[1,125,64]{1,2,0:T(8,128)S(1)} %select_bitcast_fusion.10), channel_id=1, source_target_pairs={{16,0},{32,16},{48,32},{64,48},{80,64},{96,80},{112,96},{128,112},... | collective-permute-start | bytes 96008 | tf_op jit(solution)/shard_map/ppermute | solution.py:23
  205.0 17.4 %collective-permute-start.24 = (f32[1,125,64]{1,2,0:T(8,128)S(1)}, f32[1,125,64]{1,2,0:T(8,128)S(1)}, u32[]{:S(2)}, u32[]{:S(2)}) collective-permute-start(f32[1,125,64]{1,2,0:T(8,128)S(1)} %select_bitcast_fusion.7), channel_id=1, source_target_pairs={{0,16},{16,32},{32,48},{48,64},{64,80},{80,96},{96,112},{112,128},... | collective-permute-start | bytes 96008 | tf_op jit(solution)/shard_map/ppermute | solution.py:21
  207.0 15.4 %collective-permute-start.25 = (f32[1,125,64]{1,2,0:T(8,128)S(1)}, f32[1,125,64]{1,2,0:T(8,128)S(1)}, u32[]{:S(2)}, u32[]{:S(2)}) collective-permute-start(f32[1,125,64]{1,2,0:T(8,128)S(1)} %select_bitcast_fusion.6), channel_id=1, source_target_pairs={{16,0},{32,16},{48,32},{64,48},{80,64},{96,80},{112,96},{128,112},... | collective-permute-start | bytes 96008 | tf_op jit(solution)/shard_map/ppermute | solution.py:23
  228.8 27.0 %collective-permute-start.28 = (f32[1,125,64]{1,2,0:T(8,128)S(1)}, f32[1,125,64]{1,2,0:T(8,128)S(1)}, u32[]{:S(2)}, u32[]{:S(2)}) collective-permute-start(f32[1,125,64]{1,2,0:T(8,128)S(1)} %select_bitcast_fusion.3), channel_id=1, source_target_pairs={{0,16},{16,32},{32,48},{48,64},{64,80},{80,96},{96,112},{112,128},... | collective-permute-start | bytes 96008 | tf_op jit(solution)/shard_map/ppermute | solution.py:21
  230.8 25.0 %collective-permute-start.29 = (f32[1,125,64]{1,2,0:T(8,128)S(1)}, f32[1,125,64]{1,2,0:T(8,128)S(1)}, u32[]{:S(2)}, u32[]{:S(2)}) collective-permute-start(f32[1,125,64]{1,2,0:T(8,128)S(1)} %select_bitcast_fusion.2), channel_id=1, source_target_pairs={{16,0},{32,16},{48,32},{64,48},{80,64},{96,80},{112,96},{128,112},... | collective-permute-start | bytes 96008 | tf_op jit(solution)/shard_map/ppermute | solution.py:23
  238.2 17.7 %collective-permute-start.30 = (f32[1,125,64]{1,2,0:T(8,128)S(1)}, f32[1,125,64]{1,2,0:T(8,128)S(1)}, u32[]{:S(2)}, u32[]{:S(2)}) collective-permute-start(f32[1,125,64]{1,2,0:T(8,128)S(1)} %select_bitcast_fusion.1), channel_id=1, source_target_pairs={{0,1},{1,2},{2,3},{3,4},{4,5},{5,6},{6,7},{7,8},{8,9},{9,10},{10,1... | collective-permute-start | bytes 96008 | tf_op jit(solution)/shard_map/ppermute | solution.py:21
  247.4 10.0 %collective-permute-start.31 = (f32[1,125,64]{1,2,0:T(8,128)S(1)}, f32[1,125,64]{1,2,0:T(8,128)S(1)}, u32[]{:S(2)}, u32[]{:S(2)}) collective-permute-start(f32[1,125,64]{1,2,0:T(8,128)S(1)} %select_bitcast_fusion), channel_id=1, source_target_pairs={{1,0},{2,1},{3,2},{4,3},{5,4},{6,5},{7,6},{8,7},{9,8},{10,9},{11,1... | collective-permute-start | bytes 96008 | tf_op jit(solution)/shard_map/ppermute | solution.py:23
  (8 other events, 62.7 us)
where the time goes:
time: 309 us; the launch traced here: 307 us
  starting transfers between devices  182 us (59%)
  local copies, waits for them, and re-layouts  48.5 us (16%)
  blocking collectives  45.6 us (15%)
  other arithmetic  16.5 us (5%)
  waiting for transfers between devices  10.6 us (3%)
    ppermute x16, starting transfers between devices, extended_2(): lax.ppermute(head, axis, [((i + 1) % count, i) for i in range(ends)])  115 us
    ppermute x16, starting transfers between devices, extended_2(): lax.ppermute(tail, axis, [(i, (i + 1) % count) for i in range(ends)])  66.8 us
    psum x5, blocking collectives, by_axis(): array = lax.psum(array, axis)  45.6 us
    gather x32, local copies, waits for them, and re-layouts, gather_margin(): packs = [jnp.take(solution, sending[side], axis=1) for side in range(4)]  22.4 us
    ppermute x16, waiting for transfers between devices, extended_2(): lax.ppermute(head, axis, [((i + 1) % count, i) for i in range(ends)])  10.5 us
    dot_general x2, other arithmetic, update(): jnp.einsum('ijf,jf->if', blocks, source, preferred_element_type=jnp.float32)  8.08 us
    cond x7, local copies, waits for them, and re-layouts  7.51 us
  transfers between devices with their start and end apart: 32, of which 7 were waited for; matrix products, arithmetic and copies ran while one was open for 2% of the time, Pallas kernels for 0%

commit v1 on v0

v1 whole, which is shorter than its diff:
```python
import functools

import jax
import jax.numpy as jnp
from jax import lax
from jax.experimental import pallas as pl
from jax.experimental.pallas import tpu as pltpu
from jax.sharding import PartitionSpec as P

MESH = pl.DeviceIdType.MESH
ROWS, FACES, HALO, SIDES = 125, 128, 64, 4
N_GX, N_GY = 32, 16
GROUP_A, GROUP_B = 16, 32
F32 = jnp.float32


def gather(x, index):
    return jnp.take_along_axis(x, index, axis=1, mode="promise_in_bounds")


def total(values):
    while len(values) > 1:
        values = [a + b for a, b in zip(values[::2], values[1::2])] + (
            [values[-1]] if len(values) % 2 else []
        )
    return values[0]


def row_sums(acc, sub):
    def merge(a, b, rows, shift):
        mine = functools.reduce(
            jnp.logical_or, [sub == r for r in rows]
        )
        return jnp.where(mine, a, b) + pltpu.roll(jnp.where(mine, b, a), shift, axis=0)

    x1 = merge(acc[0], acc[4], (0, 5, 6, 7), 4)
    x2 = merge(acc[2], acc[6], (0, 1, 2, 7), 4)
    x3 = merge(acc[1], acc[5], (0, 1, 6, 7), 4)
    x4 = merge(acc[3], acc[7], (0, 1, 2, 3), 4)
    y1 = merge(x1, x2, (0, 3, 4, 7), 2)
    y2 = merge(x3, x4, (0, 1, 4, 5), 2)
    return merge(y1, y2, (0, 2, 4, 6), 1)


def kernel(
    levels,
    rounds,
    color_ref,
    rhs_ref,
    inv_hbm,
    w_ref,
    nb_ref,
    sl_ref,
    out_ref,
    norm_ref,
    stage,
    inv,
    base,
    src,
    sol,
    own,
    lane_of,
    weight_of,
    pick_of,
    send_buf,
    halo_buf,
    squares,
    part_a,
    part_b,
    buf_a,
    buf_b,
    load_sem,
    send_sem,
    recv_sem,
    send_a,
    recv_a,
    send_b,
    recv_b,
):
    gx, gy = lax.axis_index("gx"), lax.axis_index("gy")
    core, y, x_hi = gx % 2, (gx // 2) % 8, gx // 16
    z, x_lo = gy % 8, gy // 8
    me_a = core * 8 + z
    me_b = (x_hi * 2 + x_lo) * 8 + y

    def device_a(q):
        return (gx - core + q // 8, gy - z + q % 8)

    def device_b(q):
        x, other = q // 8, q % 8
        return ((x // 2) * 16 + other * 2 + core, (x % 2) * 8 + z)

    has = (gx > 0, gx < N_GX - 1, gy > 0, gy < N_GY - 1)
    to = (gx < N_GX - 1, gx > 0, gy < N_GY - 1, gy > 0)
    receiver = ((gx + 1, gy), (gx - 1, gy), (gx, gy + 1), (gx, gy - 1))

    def load(piece):
        start = (piece // 2) * 16 + (piece % 2) * 64
        size = min(16, ROWS - start)
        return pltpu.make_async_copy(
            inv_hbm.at[pl.ds(start, size)], stage.at[pl.ds(start, size)], load_sem.at[piece]
        )

    for piece in range(8):
        load(piece).start()

    barrier = pltpu.get_barrier_semaphore()
    for d in range(SIDES):
        @pl.when(to[d])
        def _():
            pl.semaphore_signal(barrier, inc=1, device_id=receiver[d], device_id_type=MESH)

    def greet(group, me, device):
        def step(q, carry):
            @pl.when(q != me)
            def _():
                pl.semaphore_signal(barrier, inc=1, device_id=device(q), device_id_type=MESH)
            return carry
        lax.fori_loop(0, group, step, 0)

    greet(GROUP_A, me_a, device_a)
    greet(GROUP_B, me_b, device_b)

    lane = lax.broadcasted_iota(jnp.int32, (8, FACES), 1)
    sub = lax.broadcasted_iota(jnp.int32, (8, FACES), 0)
    low = lane < HALO
    zero = jnp.zeros((8, FACES), F32)
    color = jnp.full((8, FACES), color_ref[0, 0], jnp.int32)

    for d in range(SIDES):
        @pl.when(jnp.logical_not(has[d]))
        def _():
            for t in range(rounds - 1):
                halo_buf[t, d] = jnp.zeros((HALO, FACES), F32)

    for k in range(4):
        slot = jnp.broadcast_to(nb_ref[k : k + 1, :], (8, FACES))
        strength = jnp.broadcast_to(w_ref[k : k + 1, :], (8, FACES))
        lane_of[k] = slot % FACES
        lane_of[4 + k] = (slot % FACES + HALO) % FACES
        for part in range(3):
            weight_of[part * 4 + k] = jnp.where(slot // FACES == part, strength, 0.0)
    for d in range(SIDES):
        faces = jnp.broadcast_to(sl_ref[d : d + 1, :], (8, HALO))
        pick_of[d, :, 0:HALO] = faces
        pick_of[d, :, HALO:FACES] = faces

    base[pl.ds(120, 8), :] = zero
    base[pl.ds(0, ROWS), :] = rhs_ref[...]
    src[...] = base[...].astype(jnp.bfloat16).astype(F32)
    sol[...] = jnp.zeros((FACES, FACES), F32)
    squares[...] = jnp.zeros((2, 8, FACES), F32)

    def clear(r, carry):
        inv[r, pl.ds(120, 8), :] = zero
        return carry
    lax.fori_loop(0, ROWS, clear, 0)
    inv[pl.ds(ROWS, 3)] = jnp.zeros((3, FACES, FACES), F32)

    def product(block, sources):
        acc = []
        for j in range(8):
            row = block * 8 + j
            acc.append(total([inv[row, pl.ds(8 * i, 8), :] * sources[i] for i in range(16)]))
        return row_sums(acc, sub)

    def accepted(t):
        first, second = levels
        return color_in(first, t), color_in(second, t)

    def color_in(table, t):
        mask = None
        for c in range(4):
            hit = jnp.logical_and(color == c, jnp.full((8, FACES), t, jnp.int32) == table[c])
            mask = hit if mask is None else jnp.logical_or(mask, hit)
        return mask

    def rounds_body(t, lo, hi, pack):
        now_1, now_2 = accepted(t)
        take = jnp.logical_or(now_1, now_2)
        sources = [src[pl.ds(8 * i, 8), :] for i in range(16)]

        def step(v, dd):
            news = []
            for block in (v, v + 8):
                at = pl.ds(pl.multiple_of(block * 8, 8), 8)
                old = sol[at, :]
                candidate = product(block, sources)
                delta = jnp.where(take, candidate - old, 0.0)
                new = jnp.where(take, candidate, old)
                sol[at, :] = new
                news.append(new)
                dd = dd + delta * delta
            if pack:
                at = pl.ds(pl.multiple_of(v * 8, 8), 8)
                for d in range(SIDES):
                    here = gather(news[0], pick_of[d])
                    there = gather(news[1], pick_of[d])
                    parts = (here, there) if d % 2 == 0 else (there, here)
                    send_buf[t - 1, d, at, :] = jnp.where(low, parts[0], parts[1])
            return dd

        dd = lax.fori_loop(lo, hi, step, zero)
        squares[0] += jnp.where(now_1, dd, 0.0)
        squares[1] += jnp.where(now_2, dd, 0.0)

    def copy(t, d):
        return pltpu.make_async_remote_copy(
            src_ref=send_buf.at[t - 1, d],
            dst_ref=halo_buf.at[t - 1, d],
            send_sem=send_sem.at[t - 1, d],
            recv_sem=recv_sem.at[t - 1, d],
            device_id=receiver[d],
            device_id_type=MESH,
        )

    def send(t):
        for d in range(SIDES):
            @pl.when(to[d])
            def _():
                copy(t, d).start()

    def own_part():
        for v in range(16):
            at = pl.ds(8 * v, 8)
            mine = sol[at, :]
            terms = [weight_of[k] * gather(mine, lane_of[k]) for k in range(4)]
            own[at, :] = base[at, :] + total(terms)

    def receive(t, pair):
        for d in (2 * pair, 2 * pair + 1):
            @pl.when(has[d])
            def _():
                copy(t, d).wait_recv()

    def halo_part(t, pair, final):
        for v in range(8):
            at = pl.ds(8 * v, 8)
            before = halo_buf[t - 1, 2 * pair, at, :]
            after = halo_buf[t - 1, 2 * pair + 1, at, :]
            for half in range(2):
                where = pl.ds(8 * v + 64 * half, 8)
                both = jnp.where(low, before, after) if half == 0 else jnp.where(low, after, before)
                terms = [
                    weight_of[4 + 4 * pair + k] * gather(both, lane_of[4 * half + k])
                    for k in range(4)
                ]
                value = own[where, :] + total(terms)
                if final:
                    src[where, :] = value.astype(jnp.bfloat16).astype(F32)
                else:
                    own[where, :] = value

    for q in range(4):
        for piece in (2 * q, 2 * q + 1):
            load(piece).wait()
            start = (piece // 2) * 16 + (piece % 2) * 64
            size = min(16, ROWS - start)

            def widen(r, carry):
                inv[r, pl.ds(0, ROWS), :] = stage[r].astype(F32)
                return carry
            lax.fori_loop(start, start + size, widen, 0)
        rounds_body(1, 2 * q, 2 * q + 2, True)

    beside = jnp.minimum(gx, 1) + jnp.minimum(N_GX - 1 - gx, 1)
    beside += jnp.minimum(gy, 1) + jnp.minimum(N_GY - 1 - gy, 1)
    pl.semaphore_wait(barrier, beside + (GROUP_A - 1 + GROUP_B - 1))

    send(1)
    own_part()

    def middle(t, carry):
        for pair in range(2):
            receive(t - 1, pair)
            halo_part(t - 1, pair, pair == 1)
        rounds_body(t, 0, 8, True)
        send(t)
        own_part()
        return carry
    lax.fori_loop(2, rounds, middle, 0)

    for pair in range(2):
        receive(rounds - 1, pair)
        halo_part(rounds - 1, pair, pair == 1)
    rounds_body(rounds, 0, 8, False)

    def exchange(value, part, buf, group, me, device, send_s, recv_s):
        part[...] = value
        buf[me] = value

        def copy_to(q):
            return pltpu.make_async_remote_copy(
                src_ref=part,
                dst_ref=buf.at[me],
                send_sem=send_s.at[q],
                recv_sem=recv_s.at[me],
                device_id=device(q),
                device_id_type=MESH,
            )

        def copy_from(q):
            return pltpu.make_async_remote_copy(
                src_ref=part,
                dst_ref=buf.at[q],
                send_sem=send_s.at[q],
                recv_sem=recv_s.at[q],
                device_id=device(q),
                device_id_type=MESH,
            )

        def others(act):
            def step(q, carry):
                @pl.when(q != me)
                def _():
                    act(q)
                return carry
            lax.fori_loop(0, group, step, 0)

        others(lambda q: copy_to(q).start())
        return others, copy_to, copy_from

    mine = jnp.concatenate(
        [jnp.sum(squares[0], axis=0, keepdims=True), jnp.sum(squares[1], axis=0, keepdims=True)], axis=0
    )
    others_a, to_a, from_a = exchange(mine, part_a, buf_a, GROUP_A, me_a, device_a, send_a, recv_a)
    out_ref[...] = sol[pl.ds(0, ROWS), :]
    others_a(lambda q: from_a(q).wait_recv())
    line = total([buf_a[q] for q in range(GROUP_A)])
    others_b, to_b, from_b = exchange(line, part_b, buf_b, GROUP_B, me_b, device_b, send_b, recv_b)
    for d in range(SIDES):
        @pl.when(to[d])
        def _():
            def step(t, carry):
                copy(t, d).wait_send()
                return carry
            lax.fori_loop(1, rounds, step, 0)
    others_a(lambda q: to_a(q).wait_send())
    others_b(lambda q: from_b(q).wait_recv())
    whole = jnp.sum(total([buf_b[q] for q in range(GROUP_B)]), axis=1, keepdims=True)
    norm_ref[...] = jnp.broadcast_to(jnp.sqrt(whole), (2, FACES))
    others_b(lambda q: to_b(q).wait_send())


def sweep_call(levels, rounds, collective_id):
    vmem, dma = pltpu.VMEM, pltpu.SemaphoreType.DMA
    square = vmem((FACES, FACES), F32)
    whole = pl.BlockSpec(memory_space=pltpu.VMEM)
    return pl.pallas_call(
        functools.partial(kernel, levels, rounds),
        out_shape=(
            jax.ShapeDtypeStruct((ROWS, FACES), F32),
            jax.ShapeDtypeStruct((2, FACES), F32),
        ),
        in_specs=[
            pl.BlockSpec(memory_space=pltpu.SMEM),
            whole,
            pl.BlockSpec(memory_space=pl.ANY),
            whole,
            whole,
            whole,
        ],
        out_specs=(whole, whole),
        scratch_shapes=[
            vmem((ROWS, ROWS, FACES), jnp.bfloat16),
            vmem((FACES, FACES, FACES), F32),
            square,
            square,
            square,
            square,
            vmem((8, 8, FACES), jnp.int32),
            vmem((12, 8, FACES), F32),
            vmem((SIDES, 8, FACES), jnp.int32),
            vmem((rounds - 1, SIDES, HALO, FACES), F32),
            vmem((rounds - 1, SIDES, HALO, FACES), F32),
            vmem((2, 8, FACES), F32),
            vmem((2, FACES), F32),
            vmem((2, FACES), F32),
            vmem((GROUP_A, 2, FACES), F32),
            vmem((GROUP_B, 2, FACES), F32),
            dma((8,)),
            dma((rounds - 1, SIDES)),
            dma((rounds - 1, SIDES)),
            dma((GROUP_A,)),
            dma((GROUP_A,)),
            dma((GROUP_B,)),
            dma((GROUP_B,)),
        ],
        compiler_params=pltpu.CompilerParams(
            collective_id=collective_id, has_side_effects=True
        ),
    )


CHAIN = ((1, 2, 3, 4), (5, 6, 7, 8))


def body(rhs, inverse, weights, neighbours, send_lists, coloring):
    solved, norms = sweep_call(CHAIN, 8, 0)(
        coloring, rhs[0], inverse[0], weights[0], neighbours[0], send_lists[0]
    )
    return solved[None], norms[:, 0]


def solution(mesh):
    in_specs = (
        P("gx", None, "gy"),
        P("gx", None, None, "gy"),
        P("gx", None, "gy"),
        P("gx", None, "gy"),
        P("gx", None, "gy"),
        P("gx", "gy"),
    )
    out_specs = (P("gx", None, "gy"), P())
    return jax.shard_map(body, mesh=mesh, in_specs=in_specs, out_specs=out_specs, check_vma=False)
```

time: 309 us -> 74.5 us (0.24)
  starting transfers between devices: 182 us -> 0 us
  Pallas kernels: 0 us -> 68.7 us
  blocking collectives: 45.6 us -> 0 us
  local copies, waits for them, and re-layouts: 48.5 us -> 4.27 us
  other arithmetic: 16.5 us -> 0 us
  waiting for transfers between devices: 10.6 us -> 0 us
    ppermute x32 -> x0, starting transfers between devices: 182 us -> none  [the longest x16 115 us: extended_2(): lax.ppermute(head, axis, [((i + 1) % count, i) for i in range(ends)])]
    pallas_call x0 -> x1, Pallas kernels: none -> 68.7 us  [body(): sweep_call(CHAIN, 8, 0)]
    psum x5 -> x0, blocking collectives: 45.6 us -> none  [by_axis(): array = lax.psum(array, axis)]
    gather x40 -> x0, local copies, waits for them, and re-layouts: 27.6 us -> none  [the longest x32 22.4 us: gather_margin(): packs = [jnp.take(solution, sending[side], axis=1) for side in range(4)]]
    cond x13 -> x0, local copies, waits for them, and re-layouts: 13.1 us -> none
    ppermute x32 -> x0, waiting for transfers between devices: 10.6 us -> none  [the longest x16 10.5 us: extended_2(): lax.ppermute(head, axis, [((i + 1) % count, i) for i in range(ends)])]
    dot_general x2 -> x0, other arithmetic: 8.08 us -> none  [update(): jnp.einsum('ijf,jf->if', blocks, source, preferred_element_type=jnp.float32)]
  transfers between devices with their start and end apart: 32 -> 0, of which waited for: 7 -> 0; matrix products, arithmetic and copies ran while one was open for 2% -> 0% of each run, Pallas kernels for 0% -> 0%
where the time goes in v1:
time: 74.5 us; the launch traced here: 74.2 us
  Pallas kernels  68.7 us (92%)
  local copies, waits for them, and re-layouts  4.27 us (6%)
  between operations  1.29 us (2%)
    pallas_call x1, Pallas kernels, body(): sweep_call(CHAIN, 8, 0)  68.7 us
    unnamed x2, local copies, waits for them, and re-layouts  2.99 us

profile of v1, /device:TPU:6, one launch (start us, length us, event | category | flops | bytes accessed | tf_op | source)
XLA Modules:
  0.0 74.2 jit_solution(13397407618209780255)
XLA Ops:
  1.3 1.5 %copy.12 = f32[1,125,128]{2,1,0:T(8,128)} copy(f32[1,125,128]{2,0,1:T(1,128)} %param.6) | data formatting | bytes 128000
  2.7 68.7 %shard_map.77 = (f32[125,128]{1,0:T(8,128)}, f32[2,128]{1,0:T(2,128)}) custom-call(s32[1,1]{1,0:T(1,128)S(6)} %copy.13.color_ref, f32[125,128]{1,0:T(8,128)} %bitcast.9, bf16[125,125,128]{2,1,0:T(8,128)(2,1)} %bitcast.8, f32[4,128]{1,0:T(4,128)} %bitcast.11, s32[4,128]{1,0:T(4,128)} %bitcast.12, s32[4,64]{1,0:T(4,128)} %bitcast.13), custom_call_target="tpu_custom_call" | custom-call | tf_op jit(solution)/shard_map/pallas_call | solution.py:399
  71.4 1.5 %copy.9 = f32[1,125,128]{2,0,1:T(1,128)} copy(f32[1,125,128]{2,1,0:T(8,128)} %bitcast.10) | data formatting | bytes 128000
  72.9 1.3 %slice_reduce_fusion = f32[2]{0:T(128)} fusion(f32[2,128]{1,0:T(2,128)} %get-tuple-element.5), kind=kLoop, calls=%fused_computation.1 | loop fusion | bytes 16 | tf_op jit(solution)/shard_map/slice | solution.py:402
